TPU v7x, 32 devices: a whole 2x2x4 slice. The times are simulated.
32 devices in a mesh: groups: 2 (over y), seq: 8 (over z, x), tensor: 2 (over core).
Axes of the slice: x: 2, y: 2, z: 4, core: 2. Of those that a mesh axis runs over, the one named last changes fastest.
Arguments:
- queries: bfloat16 [2048, 1536], P(('groups', 'seq'), 'tensor'), parts along dimension 0, may hold values from -64 to 64
- keys: bfloat16 [2048, 1536], P(('groups', 'seq'), 'tensor'), parts along dimension 0, may hold values from -6 to 6
- values: bfloat16 [2048, 1536], P(('groups', 'seq'), 'tensor'), parts along dimension 0, may hold values from -6 to 6
- text_keys: bfloat16 [64, 1536], P(('groups', 'seq'), 'tensor'), parts along dimension 0, may hold values from -6 to 6
- text_values: bfloat16 [64, 1536], P(('groups', 'seq'), 'tensor'), parts along dimension 0, may hold values from -6 to 6
- conv_weight: bfloat16 [4, 1536], P(None, 'tensor'), may hold values from -3 to 3
- out_weight: bfloat16 [1536, 1536], P('tensor'), may hold values from -0.15625 to 0.15625
- image_hidden: bfloat16 [2048, 1536], P(('groups', 'seq')), parts along dimension 0, may hold values from -6 to 6
- gate: bfloat16 [3072], P('groups'), parts along dimension 0, may hold values from -8 to 8
Outputs:
- mixed: bfloat16 [2048, 1536], P(('groups', 'seq')), parts along dimension 0
There are 2 independent parts, one for each index of `groups`. A program takes and returns all parts, laid end to end along the dimension named above; an argument that names none is the same for every part. Nothing has to cross between parts.
All inputs are finite; a program needn't handle non-finite values.
Results may differ from a plain program's by a relative error of at most 0.011.
Values may be sent and summed in bfloat16 or wider, within the bound.
A program may use at most 64 MiB of HBM per device.

v0:
```python
import math
import jax
import jax.numpy as jnp
from jax import lax
from jax.sharding import PartitionSpec as P

HEAD_DIM = 128
key_block = 512


def rope_angles(row_pos, col_pos, head_dim):
    lead_dims = head_dim // 8
    group_dims = head_dim * 7 // 16
    frequency = 10000.0 ** (-(2.0 * jnp.arange(group_dims // 2, dtype=jnp.float32)) / group_dims)
    zero_angles = jnp.zeros((row_pos.shape[0], lead_dims // 2), jnp.float32)
    return jnp.concatenate(
        [zero_angles, row_pos[:, None] * frequency[None, :], col_pos[:, None] * frequency[None, :]],
        axis=1,
    )


def apply_rope(field, angles):
    paired = field.reshape(field.shape[0], field.shape[1], field.shape[2] // 2, 2)
    even_part = paired[..., 0]
    odd_part = paired[..., 1]
    cos_part = jnp.cos(angles)[:, None, :]
    sin_part = jnp.sin(angles)[:, None, :]
    turned = jnp.stack(
        [even_part * cos_part - odd_part * sin_part, even_part * sin_part + odd_part * cos_part],
        axis=-1,
    )
    return turned.reshape(field.shape)


def compress(field, taps, row_width):
    features = field.shape[1]
    grid_cells = field.astype(jnp.float32).reshape(2, row_width // 2, 2, features)
    tap_grid = taps.astype(jnp.float32).reshape(2, 2, features)
    return (
        grid_cells[0, :, 0] * tap_grid[0, 0]
        + grid_cells[0, :, 1] * tap_grid[0, 1]
        + grid_cells[1, :, 0] * tap_grid[1, 0]
        + grid_cells[1, :, 1] * tap_grid[1, 1]
    )


def absorb_block(carry, key_rows, value_rows, queries_rot):
    row_max, row_total, accumulated = carry
    heads_dev = queries_rot.shape[1]
    key_heads = key_rows.reshape(key_rows.shape[0], heads_dev, -1)
    value_heads = value_rows.reshape(value_rows.shape[0], heads_dev, -1)
    scores = jnp.einsum(
        "qhd,khd->hqk", queries_rot, key_heads, preferred_element_type=jnp.float32
    ) * (1.0 / math.sqrt(HEAD_DIM))
    new_max = jnp.maximum(row_max, jnp.max(scores, axis=-1))
    rescale = jnp.exp(row_max - new_max)
    weights = jnp.exp(scores - new_max[:, :, None]).astype(jnp.bfloat16)
    row_total = row_total * rescale + jnp.sum(weights.astype(jnp.float32), axis=-1)
    mixed_values = jnp.einsum(
        "hqk,khd->qhd", weights, value_heads, preferred_element_type=jnp.float32
    )
    accumulated = accumulated * rescale.T[:, :, None] + mixed_values
    return (new_max, row_total, accumulated)


def absorb(carry, key_rows, value_rows, queries_rot):
    key_count = key_rows.shape[0]
    if key_count > key_block and key_count % key_block == 0:
        stacked_keys = key_rows.reshape(key_count // key_block, key_block, key_rows.shape[1])
        stacked_values = value_rows.reshape(key_count // key_block, key_block, value_rows.shape[1])

        def one_step(running, block_pair):
            return (absorb_block(running, block_pair[0], block_pair[1], queries_rot), None)

        carry, unused = lax.scan(one_step, carry, (stacked_keys, stacked_values))
        return carry
    return absorb_block(carry, key_rows, value_rows, queries_rot)


def local(
    queries, keys, values, text_keys, text_values, conv_weight, out_weight, image_hidden, gate
):
    local_tokens, features = queries.shape
    row_width = local_tokens // 2
    heads_dev = features // HEAD_DIM
    seq_place = lax.axis_index("seq").astype(jnp.float32)
    token_ids = jnp.arange(local_tokens, dtype=jnp.int32)
    query_rows = 2.0 * seq_place + (token_ids // row_width).astype(jnp.float32)
    query_cols = (token_ids % row_width).astype(jnp.float32)
    queries_rot = apply_rope(
        queries.astype(jnp.float32).reshape(local_tokens, heads_dev, HEAD_DIM),
        rope_angles(query_rows, query_cols, HEAD_DIM),
    ).astype(jnp.bfloat16)
    patch_ids = jnp.arange(row_width // 2, dtype=jnp.int32).astype(jnp.float32)
    patch_rows = 2.0 * seq_place + 0.5 + 0.0 * patch_ids
    patch_cols = 2.0 * patch_ids + 0.5
    short_keys = (
        apply_rope(
            compress(keys, conv_weight, row_width).reshape(row_width // 2, heads_dev, HEAD_DIM),
            rope_angles(patch_rows, patch_cols, HEAD_DIM),
        )
        .astype(jnp.bfloat16)
        .reshape(row_width // 2, features)
    )
    short_values = compress(values, conv_weight, row_width).astype(jnp.bfloat16)
    initial = (
        jnp.full((heads_dev, local_tokens), -1e30, jnp.float32),
        jnp.zeros((heads_dev, local_tokens), jnp.float32),
        jnp.zeros((local_tokens, heads_dev, HEAD_DIM), jnp.float32),
    )
    all_text_keys, all_text_values = (
        lax.all_gather(text_keys, "seq", axis=0, tiled=True),
        lax.all_gather(text_values, "seq", axis=0, tiled=True),
    )
    after_text = absorb(initial, all_text_keys, all_text_values, queries_rot)
    row_max, row_total, accumulated = absorb(
        after_text,
        lax.all_gather(short_keys, "seq", axis=0, tiled=True),
        lax.all_gather(short_values, "seq", axis=0, tiled=True),
        queries_rot,
    )
    attended = (
        (accumulated / row_total.T[:, :, None]).astype(jnp.bfloat16).reshape(local_tokens, features)
    )
    projected = lax.psum(
        jnp.dot(attended, out_weight, preferred_element_type=jnp.float32).astype(jnp.bfloat16),
        "tensor",
    ).astype(jnp.float32)
    return (
        image_hidden.astype(jnp.float32) + gate.astype(jnp.float32)[None, :] * projected
    ).astype(jnp.bfloat16)


def solution(mesh):
    placed = (
        P(("groups", "seq"), "tensor"),
        P(("groups", "seq"), "tensor"),
        P(("groups", "seq"), "tensor"),
        P(("groups", "seq"), "tensor"),
        P(("groups", "seq"), "tensor"),
        P(None, "tensor"),
        P("tensor", None),
        P(("groups", "seq"), None),
        P("groups"),
    )
    return jax.shard_map(
        local, mesh=mesh, in_specs=placed, out_specs=P(("groups", "seq"), None), check_vma=False
    )
```

profile of v0, /device:TPU:0, one launch (start us, length us, event | category | flops | bytes accessed | tf_op | source)
XLA Modules:
  0.0 191.8 jit_solution(10425235532652120512)
XLA Ops:
  6.5 0.0 copy-start
  6.5 0.0 all-reduce.2.cloned.1.call-start
  6.5 0.5 multiply_power_fusion
  7.1 0.6 fusion.22
  7.6 0.7 reshape.261
  8.4 0.8 mul.304
  9.2 0.8 mul.307
  10.1 0.8 mul.310
  10.9 0.8 mul.313
  11.7 1.1 reshape.259
  12.9 1.0 fusion.27
  13.8 0.2 copy.66
  14.0 0.2 copy.63
  14.2 1.1 copy.64
  15.2 1.8 copy.65
  17.0 0.6 fusion.24
  17.6 0.0 copy-start.7
  17.6 0.7 broadcast_multiply_fusion.1
  18.3 0.2 fusion.15
  18.5 0.0 copy-done.7
  18.5 3.4 %multiply_add_fusion = f32[32,6,64,2]{0,3,2,1:T(2,128)S(1)} fusion(f32[32,6,64,2]{0,3,2,1:T(2,128)S(1)} %bitcast.86, f32[32,6,64,2]{0,3,2,1:T(2,128)} %bitcast.89, f32[32,6,64,2]{0,3,2,1:T(2,128)S(1)} %bitcast.88, f32[32,6,64,2]{0,3,2,1:T(2,128)S(1)} %bitcast.87, f32[6,64,2]{2,1,0:T(8,128)} %mul.313, f32[6,64,2]{2,1,0:T(8,128)} %mul.310, ...), kind=kLoop, calls=%fused_computation.13 | loop fusion | flops 172032 | bytes 503808 | tf_op jit(solution)/shard_map/add | solution.py:40
  21.9 0.0 copy-start.4
  22.0 0.5 subtract_convert_fusion
  22.5 0.5 pad_maximum_fusion.1
  23.0 0.1 copy.51
  23.1 32.8 %all_gather.14 = bf16[256,768]{1,0:T(8,128)(2,1)S(1)} all-gather(bf16[32,768]{1,0:T(8,128)(2,1)S(1)} %copy.51), channel_id=1, replica_groups=mesh['groups'=2,'seq'=8,'tensor'=2] {'seq'}, dimensions={0}, use_global_device_ids=true | all-gather | bytes 442368 | tf_op jit(solution)/shard_map/all_gather | solution.py:118
  55.9 0.2 copy.52
  56.1 0.0 copy-done.4
  56.1 0.2 copy.43
  56.2 0.1 convert.20
  56.4 31.0 %all-gather = bf16[8,4,768]{2,1,0:T(4,128)(2,1)S(1)} all-gather(bf16[1,4,768]{2,1,0:T(4,128)(2,1)} %bitcast.93), channel_id=1, replica_groups=mesh['groups'=2,'seq'=8,'tensor'=2] {'seq'}, dimensions={0}, use_global_device_ids=true | all-gather | bytes 55296 | tf_op jit(solution)/shard_map/all_gather | solution.py:112
  87.4 0.7 reshape.246
  88.0 0.0 copy-start.3
  88.0 0.8 broadcast_multiply_fusion.3
  88.8 0.8 fusion.17
  89.6 0.5 subtract_convert_fusion.1
  90.1 0.5 pad_maximum_fusion
  90.6 1.0 fusion.30
  91.5 0.0 copy-done.3
  91.5 1.4 fusion.29
  92.9 1.1 reshape.263
  94.1 0.3 fusion.28
  94.4 0.0 copy-start.5
  94.4 31.0 %all_gather.15 = bf16[256,768]{1,0:T(8,128)(2,1)S(1)} all-gather(bf16[32,768]{1,0:T(8,128)(2,1)S(1)} %fusion.8), channel_id=1, replica_groups=mesh['groups'=2,'seq'=8,'tensor'=2] {'seq'}, dimensions={0}, use_global_device_ids=true | all-gather | bytes 442368 | tf_op jit(solution)/shard_map/all_gather | solution.py:119
  125.4 0.9 copy.58
  126.3 0.0 copy-start.2
  126.3 0.7 broadcast_maximum_fusion
  127.0 0.3 convert_reduce_fusion
  127.3 2.1 %convolution_bitcast_fusion.1 = f32[128,6,128]{0,2,1:T(8,128)} fusion(bf16[256,6,128]{0,2,1:T(8,128)(2,1)} %bitcast.85, f32[6,128,256]{2,1,0:T(8,128)S(1)} %get-tuple-element.37, f32[6,128]{1,0:T(8,128)S(1)} %get-tuple-element.29), kind=kOutput, calls=%fused_computation.4 | convolution fusion | flops 50724864 | bytes 1575936 | tf_op jit(solution)/shard_map/hqk,khd->qhd/dot_general | solution.py:59
  129.4 0.0 copy-done.5
  129.4 30.8 %all-gather.1 = bf16[8,4,768]{2,1,0:T(4,128)(2,1)S(1)} all-gather(bf16[1,4,768]{2,1,0:T(4,128)(2,1)S(1)} %bitcast.94), channel_id=1, replica_groups=mesh['groups'=2,'seq'=8,'tensor'=2] {'seq'}, dimensions={0}, use_global_device_ids=true | all-gather | bytes 55296 | tf_op jit(solution)/shard_map/all_gather | solution.py:113
  160.2 0.0 copy-done.2
  160.3 0.7 bitcast_add_fusion
  161.0 0.0 copy-start.6
  161.0 0.0 copy-start.1
  161.0 1.4 fusion.4
  162.4 0.0 copy-done
  162.4 1.2 convolution_convert_fusion
  163.6 0.0 all-reduce.2.cloned.1.call-update
  163.7 0.0 copy-done.6
  163.7 19.4 %all-reduce.2.cloned.1.call-done = bf16[128,1536]{1,0:T(8,128)(2,1)} async-done(((bf16[128,1536]{1,0:T(8,128)(2,1)}), bf16[128,1536]{1,0:T(8,128)(2,1)}) %all-reduce.2.cloned.1.call-update) | async-done | bytes 393232 | tf_op jit(solution)/shard_map/psum | solution.py:125
  183.1 0.0 copy-done.1
  183.1 1.9 add_convert_fusion
  (8 shorter events, 0.1 us)
Async XLA Ops:
  6.5 155.8 %copy-start = (bf16[768,1536]{1,0:T(8,128)(2,1)S(1)}, bf16[768,1536]{1,0:T(8,128)(2,1)}, u32[]{:S(2)}) copy-start(bf16[768,1536]{1,0:T(8,128)(2,1)} %param.15) | copy-start | bytes 7077892
  6.5 176.6 %all-reduce.2.cloned.1.call-start = ((), (), s32[]{:S(2)}) async-start(), calls=%async_computation | async-start | bytes 786432 | tf_op jit(solution)/shard_map/psum | solution.py:125
  17.6 0.9 copy-start.7
  21.9 34.1 %copy-start.4 = (bf16[128,768]{1,0:T(8,128)(2,1)S(1)}, bf16[128,768]{1,0:T(8,128)(2,1)}, u32[]{:S(2)}) copy-start(bf16[128,768]{1,0:T(8,128)(2,1)} %param.9) | copy-start | bytes 589828
  88.0 3.5 %copy-start.3 = (bf16[32,6,128]{2,1,0:T(8,128)(2,1)S(1)}, bf16[32,6,128]{2,1,0:T(8,128)(2,1)}, u32[]{:S(2)}) copy-start(bf16[32,6,128]{2,1,0:T(8,128)(2,1)} %reshape.246) | copy-start | bytes 147460
  94.4 35.0 %copy-start.5 = (bf16[4,768]{1,0:T(4,128)(2,1)S(1)}, bf16[4,768]{1,0:T(4,128)(2,1)}, u32[]{:S(2)}) copy-start(bf16[4,768]{1,0:T(4,128)(2,1)} %param.13) | copy-start | bytes 18436
  126.3 33.9 %copy-start.2 = (f32[6,128,32]{1,2,0:T(8,128)S(1)}, f32[6,128,32]{1,2,0:T(8,128)}, u32[]{:S(2)}) copy-start(f32[6,128,32]{1,2,0:T(8,128)} %get-tuple-element.35) | copy-start | bytes 294916
  161.0 2.7 %copy-start.6 = (bf16[1536]{0:T(1024)(128)(2,1)S(1)}, bf16[1536]{0:T(1024)(128)(2,1)}, u32[]{:S(2)}) copy-start(bf16[1536]{0:T(1024)(128)(2,1)} %param.17) | copy-start | bytes 9220
  161.0 22.1 %copy-start.1 = (bf16[128,1536]{1,0:T(8,128)(2,1)S(1)}, bf16[128,1536]{1,0:T(8,128)(2,1)}, u32[]{:S(2)}) copy-start(bf16[128,1536]{1,0:T(8,128)(2,1)} %param.16) | copy-start | bytes 1179652
Sparse Core Ops, SparseCore 0:
  163.8 19.2 all-reduce.1
where the time goes:
time: 192 us
  blocking collectives  125 us (65%)
  waiting for transfers between devices  19.4 us (10%)
  between operations  13.6 us (7%)
  other arithmetic  13.3 us (7%)
  local copies, waits for them, and re-layouts  12.9 us (7%)
  matrix products  7.08 us (4%)
    all_gather x1, blocking collectives, local(): lax.all_gather(short_keys, 'seq', axis=0, tiled=True)  32.8 us
    all_gather x1, blocking collectives, local(): lax.all_gather(text_keys, 'seq', axis=0, tiled=True)  31 us
    all_gather x1, blocking collectives, local(): lax.all_gather(short_values, 'seq', axis=0, tiled=True)  31 us
    all_gather x1, blocking collectives, local(): lax.all_gather(text_values, 'seq', axis=0, tiled=True)  30.8 us
    psum x1, waiting for transfers between devices, local(): lax.psum(jnp.dot(attended, out_weight, preferred_element_type=jnp.float32...  19.4 us
  transfers between devices with their start and end apart: 1, of which 1 were waited for; matrix products, arithmetic and copies ran while one was open for 0% of the time, Pallas kernels for 0%

commit v1 on v0

--- a/solution.py
+++ b/solution.py
@@ -122,9 +122,12 @@
     attended = (
         (accumulated / row_total.T[:, :, None]).astype(jnp.bfloat16).reshape(local_tokens, features)
     )
-    projected = lax.psum(
-        jnp.dot(attended, out_weight, preferred_element_type=jnp.float32).astype(jnp.bfloat16),
-        "tensor",
+    projected = jnp.sum(
+        lax.all_gather(
+            jnp.dot(attended, out_weight, preferred_element_type=jnp.float32).astype(jnp.bfloat16),
+            "tensor",
+        ),
+        axis=0,
     ).astype(jnp.float32)
     return (
         image_hidden.astype(jnp.float32) + gate.astype(jnp.float32)[None, :] * projected

time: 192 us -> 158 us (0.82)
  waiting for transfers between devices: 19.4 us -> 0 us
  between operations: 13.6 us -> 0.28 us
  other arithmetic: 13.3 us -> 9.89 us
  blocking collectives: 125 us -> 128 us
  matrix products: 7.08 us -> 4.57 us
  local copies, waits for them, and re-layouts: 12.9 us -> 15.4 us
    psum x1 -> x0, waiting for transfers between devices: 19.4 us -> none  [local(): lax.psum(jnp.dot(attended, out_weight, preferred_element_type=jnp.float32...]
    all_gather x0 -> x1, blocking collectives: none -> 2.37 us  [local(): lax.all_gather(jnp.dot(attended, out_weight, preferred_element_type=jnp.f...]
    unnamed x21 -> x23, local copies, waits for them, and re-layouts: 3.42 us -> 5.64 us
  transfers between devices with their start and end apart: 1 -> 0, of which waited for: 1 -> 0; matrix products, arithmetic and copies ran while one was open for 0% -> 0% of each run, Pallas kernels for 0% -> 0%
where the time goes in v1:
time: 158 us
  blocking collectives  128 us (81%)
  local copies, waits for them, and re-layouts  15.4 us (10%)
  other arithmetic  9.89 us (6%)
  matrix products  4.57 us (3%)
    all_gather x1, blocking collectives, local(): lax.all_gather(short_keys, 'seq', axis=0, tiled=True)  32.8 us
    all_gather x1, blocking collectives, local(): lax.all_gather(short_values, 'seq', axis=0, tiled=True)  31 us
    all_gather x1, blocking collectives, local(): lax.all_gather(text_keys, 'seq', axis=0, tiled=True)  30.8 us
    all_gather x1, blocking collectives, local(): lax.all_gather(text_values, 'seq', axis=0, tiled=True)  30.8 us
    unnamed x23, local copies, waits for them, and re-layouts  5.64 us
    add x1, other arithmetic, compress(): grid_cells[0, :, 0] * tap_grid[0, 0] + grid_cells[0, :, 1] * tap_grid[0, 1]  3.48 us

profile of v1, /device:TPU:0, one launch (start us, length us, event | category | flops | bytes accessed | tf_op | source)
XLA Modules:
  0.0 157.8 jit_solution(3511188058106103889)
XLA Ops:
  0.0 0.0 copy-start
  0.0 0.9 reshape.261
  0.9 0.0 copy-start.3
  0.9 0.8 mul.304
  1.7 0.8 mul.307
  2.6 0.8 mul.310
  3.4 0.0 copy-done.3
  3.4 0.8 mul.313
  4.3 1.1 reshape.259
  5.4 1.0 fusion.27
  6.4 0.2 copy.66
  6.5 1.1 copy.63
  7.6 1.8 %copy.64 = f32[1,32,1,768]{1,3,2,0:T(8,128)} copy(f32[1,32,1,768]{3,2,1,0:T(1,128)} %get-tuple-element.17) | data formatting | bytes 196608
  9.4 1.8 %copy.65 = f32[1,32,1,768]{1,3,2,0:T(8,128)} copy(f32[1,32,1,768]{3,2,1,0:T(1,128)} %get-tuple-element.16) | data formatting | bytes 196608
  11.2 3.5 %multiply_add_fusion = f32[32,6,64,2]{0,3,2,1:T(2,128)S(1)} fusion(f32[32,6,64,2]{0,3,2,1:T(2,128)S(1)} %bitcast.88, f32[32,6,64,2]{0,3,2,1:T(2,128)} %bitcast.91, f32[32,6,64,2]{0,3,2,1:T(2,128)} %bitcast.90, f32[32,6,64,2]{0,3,2,1:T(2,128)S(1)} %bitcast.89, f32[6,64,2]{2,1,0:T(8,128)} %mul.313, f32[6,64,2]{2,1,0:T(8,128)} %mul.310, f32[6,64,2]{2,1,0:T(8,128)} %mul.307, ...), kind=kLoop, calls=%fused_computation.13 | loop fusion | flops 172032 | bytes 503808 | tf_op jit(solution)/shard_map/add | solution.py:40
  14.7 0.0 copy-start.2
  14.8 0.1 broadcast_multiply_fusion.1
  14.8 0.2 fusion.15
  15.0 0.5 subtract_convert_fusion
  15.6 0.5 pad_maximum_fusion.1
  16.1 0.1 copy.51
  16.2 32.8 %all_gather.20 = bf16[256,768]{1,0:T(8,128)(2,1)S(1)} all-gather(bf16[32,768]{1,0:T(8,128)(2,1)S(1)} %copy.51), channel_id=1, replica_groups=mesh['groups'=2,'seq'=8,'tensor'=2] {'seq'}, dimensions={0}, use_global_device_ids=true | all-gather | bytes 442368 | tf_op jit(solution)/shard_map/all_gather | solution.py:118
  49.0 0.0 copy-start.6
  49.0 0.9 copy.52
  49.9 0.1 broadcast_multiply_fusion.3
  50.0 0.2 fusion.17
  50.2 0.0 copy-done.2
  50.2 0.2 copy.43
  50.4 0.1 convert.21
  50.5 0.5 subtract_convert_fusion.1
  51.0 0.5 pad_maximum_fusion
  51.5 1.4 fusion.30
  52.9 0.0 copy-done.6
  52.9 30.8 %all-gather.1 = bf16[8,4,768]{2,1,0:T(4,128)(2,1)S(1)} all-gather(bf16[1,4,768]{2,1,0:T(4,128)(2,1)S(1)} %bitcast.95), channel_id=1, replica_groups=mesh['groups'=2,'seq'=8,'tensor'=2] {'seq'}, dimensions={0}, use_global_device_ids=true | all-gather | bytes 55296 | tf_op jit(solution)/shard_map/all_gather | solution.py:112
  83.7 0.2 fusion.29
  83.9 0.0 copy-start.1
  83.9 0.0 copy-start.4
  83.9 0.6 copy-done.1
  84.5 0.0 copy-done.4
  84.5 0.3 convert_reduce_fusion
  84.9 0.6 bitcast_add_fusion
  85.5 1.1 reshape.263
  86.6 0.3 fusion.28
  86.9 0.7 fusion.8
  87.6 0.0 copy-start.7
  87.6 0.0 copy-start.5
  87.6 31.0 %all_gather.21 = bf16[256,768]{1,0:T(8,128)(2,1)S(1)} all-gather(bf16[32,768]{1,0:T(8,128)(2,1)S(1)} %fusion.8), channel_id=1, replica_groups=mesh['groups'=2,'seq'=8,'tensor'=2] {'seq'}, dimensions={0}, use_global_device_ids=true | all-gather | bytes 442368 | tf_op jit(solution)/shard_map/all_gather | solution.py:119
  118.6 0.9 copy.58
  119.5 1.3 convolution_bitcast_fusion.1
  120.9 0.0 copy-done.7
  120.9 30.8 %all-gather.2 = bf16[8,4,768]{2,1,0:T(4,128)(2,1)S(1)} all-gather(bf16[1,4,768]{2,1,0:T(4,128)(2,1)S(1)} %bitcast.96), channel_id=1, replica_groups=mesh['groups'=2,'seq'=8,'tensor'=2] {'seq'}, dimensions={0}, use_global_device_ids=true | all-gather | bytes 55296 | tf_op jit(solution)/shard_map/all_gather | solution.py:113
  151.7 0.0 copy-done.5
  151.7 1.2 fusion.4
  152.9 0.0 copy-done
  152.9 0.0 copy-start.8
  152.9 0.5 convolution_convert_fusion
  153.4 2.4 %all-gather = bf16[256,1536]{1,0:T(8,128)(2,1)S(1)} all-gather(bf16[128,1536]{1,0:T(8,128)(2,1)S(1)} %convolution_convert_fusion), channel_id=2, replica_groups=mesh['groups'=2,'seq'=8,'tensor'=2] {'tensor'}, dimensions={0}, use_global_device_ids=true | all-gather | bytes 1179648 | tf_op jit(solution)/shard_map/all_gather | solution.py:126
  155.8 0.2 reduce_sum.38
  155.9 0.0 copy-done.8
  155.9 1.9 %add_convert_fusion = bf16[128,1536]{1,0:T(8,128)(2,1)} fusion(bf16[128,1536]{1,0:T(8,128)(2,1)S(1)} %reduce_sum.38, bf16[128,1536]{1,0:T(8,128)(2,1)} %param.16, f32[1536]{0:T(1024)S(1)} %convert_element_type.79), kind=kLoop, calls=%fused_computation.10 | loop fusion | flops 983040 | bytes 1185792 | tf_op jit(solution)/shard_map/convert_element_type | solution.py:134
  (12 shorter events, 0.2 us)
Async XLA Ops:
  0.0 152.9 %copy-start = (bf16[768,1536]{1,0:T(8,128)(2,1)S(1)}, bf16[768,1536]{1,0:T(8,128)(2,1)}, u32[]{:S(2)}) copy-start(bf16[768,1536]{1,0:T(8,128)(2,1)} %param.15) | copy-start | bytes 7077892
  0.9 2.5 %copy-start.3 = (f32[768]{0:T(1024)}, f32[768]{0:T(1024)S(1)}, u32[]{:S(2)}) copy-start(f32[768]{0:T(1024)S(1)} %get-tuple-element.8) | copy-start | bytes 9220
  14.7 35.5 %copy-start.2 = (bf16[128,768]{1,0:T(8,128)(2,1)S(1)}, bf16[128,768]{1,0:T(8,128)(2,1)}, u32[]{:S(2)}) copy-start(bf16[128,768]{1,0:T(8,128)(2,1)} %param.9) | copy-start | bytes 589828
  49.0 3.9 %copy-start.6 = (bf16[4,768]{1,0:T(4,128)(2,1)S(1)}, bf16[4,768]{1,0:T(4,128)(2,1)}, u32[]{:S(2)}) copy-start(bf16[4,768]{1,0:T(4,128)(2,1)} %param.12) | copy-start | bytes 18436
  83.9 0.6 copy-start.1
  83.9 0.6 copy-start.4
  87.6 33.3 %copy-start.7 = (bf16[4,768]{1,0:T(4,128)(2,1)S(1)}, bf16[4,768]{1,0:T(4,128)(2,1)}, u32[]{:S(2)}) copy-start(bf16[4,768]{1,0:T(4,128)(2,1)} %param.13) | copy-start | bytes 18436
  87.6 64.1 %copy-start.5 = (f32[6,128]{1,0:T(8,128)S(1)}, f32[6,128]{1,0:T(8,128)}, u32[]{:S(2)}) copy-start(f32[6,128]{1,0:T(8,128)} %copy-done.4) | copy-start | bytes 9220
  152.9 3.0 %copy-start.8 = (bf16[1536]{0:T(1024)(128)(2,1)S(1)}, bf16[1536]{0:T(1024)(128)(2,1)}, u32[]{:S(2)}) copy-start(bf16[1536]{0:T(1024)(128)(2,1)} %param.17) | copy-start | bytes 9220
